TPU v7x, 32 devices: a whole 2x2x4 slice. The times are simulated.
32 devices in a mesh: rows: 2 (over y), seq: 16 (over z, x, core).
Axes of the slice: x: 2, y: 2, z: 4, core: 2. Of those that a mesh axis runs over, the one named last changes fastest.
Arguments:
- frames: bfloat16 [2, 2048, 768], P('rows', 'seq'), may hold values from -6 to 6
- segment_ids: int32 [2, 2048], P('rows', 'seq'), may hold values from 0 to 7, never falling along the last dimension, each value on 1 to 1024 neighbouring positions
- qkv_weight: bfloat16 [768, 2304], replicated, may hold values from -0.21875 to 0.21875
- query_bias: float32 [768], replicated, may hold values from -3 to 3
- value_bias: float32 [768], replicated, may hold values from -0.3125 to 0.3125
- out_weight: bfloat16 [768, 768], replicated, may hold values from -3.5 to 3.5
- out_bias: float32 [768], replicated, may hold values from -3 to 3
- norm1_gain: float32 [768], replicated, may hold values from 0.5 to 1.5
- norm1_shift: float32 [768], replicated, may hold values from -3 to 3
- up_weight: bfloat16 [768, 3072], replicated, may hold values from -0.21875 to 0.21875
- up_bias: float32 [3072], replicated, may hold values from -3 to 3
- down_weight: bfloat16 [3072, 768], replicated, may hold values from -0.109375 to 0.109375
- down_bias: float32 [768], replicated, may hold values from -3 to 3
- norm2_gain: float32 [768], replicated, may hold values from 0.5 to 1.5
- norm2_shift: float32 [768], replicated, may hold values from -3 to 3
- cotangent: bfloat16 [2, 2048, 768], P('rows', 'seq'), may hold values from -6 to 6
Outputs:
- layer_out: bfloat16 [2, 2048, 768], P('rows', 'seq')
- input_grad: float32 [2, 2048, 768], P('rows', 'seq')
- qkv_gradient: float32 [768, 2304], P(('rows', 'seq'))
- querybias_gradient: float32 [768], P(('rows', 'seq'))
- valuebias_gradient: float32 [768], P(('rows', 'seq'))
- out_gradient: float32 [768, 768], P(('rows', 'seq'))
- outbias_gradient: float32 [768], P(('rows', 'seq'))
- gain1_gradient: float32 [768], P(('rows', 'seq'))
- shift1_gradient: float32 [768], P(('rows', 'seq'))
- up_gradient: float32 [768, 3072], P(('rows', 'seq'))
- upbias_gradient: float32 [3072], P(('rows', 'seq'))
- down_gradient: float32 [3072, 768], P(('rows', 'seq'))
- downbias_gradient: float32 [768], P(('rows', 'seq'))
- gain2_gradient: float32 [768], P(('rows', 'seq'))
- shift2_gradient: float32 [768], P(('rows', 'seq'))
Inputs may be any that keep to these rules, and one draw needn't show every extreme that they name: `segment_ids`: along each row the ids never fall; each clip has 1 to 1024 frames and one has exactly 1024.
All inputs are finite; a program needn't handle non-finite values.
Results may differ from a plain program's by a relative error of at most 0.02.
Values may be sent and summed in bfloat16 or wider, within the bound.
A program may use at most 192 MiB of HBM per device.

v0:
```python
import functools
import math
import typing

import jax
import jax.numpy as jnp
from jax import lax
from jax.experimental import pallas as pl
from jax.experimental.pallas import tpu as pltpu
from jax.sharding import PartitionSpec as P

HEADS = 12
HEAD_DIM = 64


norm_eps = 1e-05
mask_fill = -1e30


def shortened(shard):

    def short(part):
        return part.astype(jnp.bfloat16) if part.dtype == jnp.float32 else part

    return jax.tree.map(short, shard)


def passed_along(value, axis, steps):
    count = lax.axis_size(axis)
    pairs = [(source, (source + steps) % count) for source in range(count)]
    return lax.ppermute(value, axis, pairs)


def layer_norm(resid, gain, shift):
    centred = resid - jnp.mean(resid, axis=-1, keepdims=True)
    inv_std = lax.rsqrt(jnp.mean(centred * centred, axis=-1, keepdims=True) + norm_eps)
    normed = centred * inv_std
    return (normed * gain + shift, normed, inv_std)


def norm_back(upstream, normed, inv_std, gain):
    scaled = upstream * gain
    first_mean = jnp.mean(scaled, axis=-1, keepdims=True)
    second_mean = jnp.mean(scaled * normed, axis=-1, keepdims=True)
    grad_in = inv_std * (scaled - first_mean - normed * second_mean)
    return (grad_in, jnp.sum(upstream * normed, axis=0), jnp.sum(upstream, axis=0))


def gelu_slope(pre_act):
    normal_cdf = 0.5 * (1.0 + lax.erf(pre_act * 0.5**0.5))
    normal_pdf = jnp.exp(-0.5 * pre_act * pre_act) * (2.0 * math.pi) ** (-0.5)
    return normal_cdf + pre_act * normal_pdf


def head_groups(head_count):
    return [(0, head_count, 1)]


def pass_keys(blocks):
    return jax.tree.map(
        lambda part, own: part.astype(own.dtype), passed_along(shortened(blocks), "seq", 1), blocks
    )


def pass_again(blocks):
    return jax.tree.map(
        lambda part, own: part.astype(own.dtype), passed_along(shortened(blocks), "seq", 1), blocks
    )


def pass_grads(blocks):
    return (
        passed_along(blocks[0].astype(jnp.bfloat16), "seq", 1).astype(jnp.float32),
        passed_along(blocks[1].astype(jnp.bfloat16), "seq", 1).astype(jnp.float32),
    )


def block_scores(query_part, key_part, query_ids, key_ids):
    scores = jnp.einsum(
        "qhe,khe->hqk", query_part, key_part, preferred_element_type=jnp.float32
    ) * HEAD_DIM ** (-0.5)
    return jnp.where((query_ids[:, None] == key_ids[None, :])[None], scores, mask_fill)


def attend_block(carried, query_part, key_part, value_part, query_ids, key_ids):
    run_max, run_total, run_acc = carried
    scores = block_scores(query_part, key_part, query_ids, key_ids)
    new_max = jnp.maximum(run_max, jnp.max(scores, axis=-1))
    weights = jnp.exp(scores - new_max[:, :, None])
    factor = jnp.exp(run_max - new_max)
    new_total = run_total * factor + jnp.sum(weights, axis=-1)
    update = jnp.einsum(
        "hqk,khe->qhe", weights.astype(jnp.bfloat16), value_part, preferred_element_type=jnp.float32
    )
    return (new_max, new_total, run_acc * factor.T[:, :, None] + update)


def grad_block(
    carried,
    query_part,
    key_part,
    value_part,
    query_ids,
    key_ids,
    context_part,
    log_part,
    delta_part,
):
    query_acc, key_acc, value_acc = carried
    scores = block_scores(query_part, key_part, query_ids, key_ids)
    probs = jnp.exp(scores - log_part[:, :, None])
    prob_grad = jnp.einsum(
        "qhe,khe->hqk", context_part, value_part, preferred_element_type=jnp.float32
    )
    score_grad = (probs * (prob_grad - delta_part[:, :, None])).astype(jnp.bfloat16)
    scale = HEAD_DIM ** (-0.5)
    query_acc = query_acc + scale * jnp.einsum(
        "hqk,khe->qhe", score_grad, key_part, preferred_element_type=jnp.float32
    )
    key_acc = key_acc + scale * jnp.einsum(
        "hqk,qhe->khe", score_grad, query_part, preferred_element_type=jnp.float32
    )
    value_acc = value_acc + jnp.einsum(
        "hqk,qhe->khe", probs.astype(jnp.bfloat16), context_part, preferred_element_type=jnp.float32
    )
    return (query_acc, key_acc, value_acc)


def forward_cycle(
    query_heads, key_heads, value_heads, local_ids, every_id, cycle_place, cycle_size
):
    frame_count, head_count, head_width = query_heads.shape
    grouping = head_groups(head_count)
    states = []
    blocks = []
    for head_first, head_last, direction in grouping:
        head_span = head_last - head_first
        initial = (
            jnp.full((head_span, frame_count), mask_fill, jnp.float32),
            jnp.zeros((head_span, frame_count), jnp.float32),
            jnp.zeros((frame_count, head_span, head_width), jnp.float32),
        )
        states.append(
            attend_block(initial, query_heads, key_heads, value_heads, local_ids, local_ids)
        )
        blocks.append((key_heads, value_heads))

    def forward_cycle_turn(turn_index, cycle_carry):
        old_states, old_blocks = cycle_carry
        new_states = []
        new_blocks = []
        for group_info, part_state, part_block in zip(grouping, old_states, old_blocks):
            head_first, head_last, direction = group_info
            part_block = pass_keys(part_block)
            source_index = (cycle_place - direction * turn_index) % cycle_size
            key_ids = lax.dynamic_slice_in_dim(every_id, source_index * frame_count, frame_count)
            new_states.append(
                attend_block(
                    part_state, query_heads, part_block[0], part_block[1], local_ids, key_ids
                )
            )
            new_blocks.append(part_block)
        return (new_states, new_blocks)

    states, blocks = lax.fori_loop(1, cycle_size, forward_cycle_turn, (states, blocks))
    maxima = jnp.concatenate([part_state[0] for part_state in states], axis=0)
    totals = jnp.concatenate([part_state[1] for part_state in states], axis=0)
    sums_all = jnp.concatenate([part_state[2] for part_state in states], axis=1)
    attended = sums_all / totals.T[:, :, None]
    return (attended, maxima + jnp.log(totals))


def backward_cycle(
    query_heads,
    key_heads,
    value_heads,
    local_ids,
    every_id,
    context_heads,
    log_total,
    row_delta,
    cycle_place,
    cycle_size,
):
    frame_count, head_count, head_width = query_heads.shape
    grouping = head_groups(head_count)
    initial = []
    for head_first, head_last, direction in grouping:
        zero_part = jnp.zeros((frame_count, head_last - head_first, head_width), jnp.float32)
        initial.append((zero_part, (key_heads, value_heads), (zero_part, zero_part)))

    def backward_cycle_turn(turn_index, cycle_carry):
        new_carry = []
        for group_info, part_carry in zip(grouping, cycle_carry):
            head_first, head_last, direction = group_info
            query_acc, part_block, part_grads = part_carry
            source_index = (cycle_place - direction * turn_index) % cycle_size
            key_ids = lax.dynamic_slice_in_dim(every_id, source_index * frame_count, frame_count)
            query_acc, key_acc, value_acc = grad_block(
                (query_acc, part_grads[0], part_grads[1]),
                query_heads,
                part_block[0],
                part_block[1],
                local_ids,
                key_ids,
                context_heads,
                log_total,
                row_delta,
            )
            part_grads = pass_grads((key_acc, value_acc))
            part_block = pass_again(part_block)
            new_carry.append((query_acc, part_block, part_grads))
        return new_carry

    final = lax.fori_loop(0, cycle_size, backward_cycle_turn, initial)
    query_grad = jnp.concatenate([part_carry[0] for part_carry in final], axis=1)
    key_grad = jnp.concatenate([part_carry[2][0] for part_carry in final], axis=1)
    value_grad = jnp.concatenate([part_carry[2][1] for part_carry in final], axis=1)
    return (query_grad, key_grad, value_grad)


def shards(
    frames,
    segment_ids,
    qkv_weight,
    query_bias,
    value_bias,
    out_weight,
    out_bias,
    norm1_gain,
    norm1_shift,
    up_weight,
    up_bias,
    down_weight,
    down_bias,
    norm2_gain,
    norm2_shift,
    cotangent,
):
    inputs = frames[0]
    local_ids = segment_ids[0]
    frame_count, model_width = inputs.shape
    cycle_size = lax.axis_size("seq")
    cycle_place = lax.axis_index("seq")
    every_id = lax.all_gather(segment_ids, "seq", axis=1, tiled=True)[0]
    head_shape = (frame_count, HEADS, HEAD_DIM)
    projected = jnp.dot(inputs, qkv_weight, preferred_element_type=jnp.float32)
    query_heads = (projected[:, :model_width] + query_bias).astype(jnp.bfloat16).reshape(head_shape)
    key_heads = projected[:, model_width : 2 * model_width].astype(jnp.bfloat16).reshape(head_shape)
    value_heads = (
        (projected[:, 2 * model_width :] + value_bias).astype(jnp.bfloat16).reshape(head_shape)
    )
    attended, log_total = forward_cycle(
        query_heads, key_heads, value_heads, local_ids, every_id, cycle_place, cycle_size
    )
    context = attended.astype(jnp.bfloat16).reshape(frame_count, model_width)
    resid_one = (
        inputs.astype(jnp.float32)
        + jnp.dot(context, out_weight, preferred_element_type=jnp.float32)
        + out_bias
    )
    hidden, normed_one, inverse_one = layer_norm(resid_one, norm1_gain, norm1_shift)
    hidden_low = hidden.astype(jnp.bfloat16)
    pre_act = jnp.dot(hidden_low, up_weight, preferred_element_type=jnp.float32) + up_bias
    act_low = jax.nn.gelu(pre_act, approximate=False).astype(jnp.bfloat16)
    resid_two = (
        hidden + jnp.dot(act_low, down_weight, preferred_element_type=jnp.float32) + down_bias
    )
    output, normed_two, inverse_two = layer_norm(resid_two, norm2_gain, norm2_shift)
    upstream = cotangent[0].astype(jnp.float32)
    second_grad, gain_two_grad, shift_two_grad = norm_back(
        upstream, normed_two, inverse_two, norm2_gain
    )
    second_low = second_grad.astype(jnp.bfloat16)
    down_grad = jnp.einsum("tf,td->fd", act_low, second_low, preferred_element_type=jnp.float32)
    pre_grad = jnp.einsum(
        "td,fd->tf", second_low, down_weight, preferred_element_type=jnp.float32
    ) * gelu_slope(pre_act)
    pre_low = pre_grad.astype(jnp.bfloat16)
    up_grad = jnp.einsum("td,tf->df", hidden_low, pre_low, preferred_element_type=jnp.float32)
    hidden_grad = second_grad + jnp.einsum(
        "tf,df->td", pre_low, up_weight, preferred_element_type=jnp.float32
    )
    first_grad, gain_one_grad, shift_one_grad = norm_back(
        hidden_grad, normed_one, inverse_one, norm1_gain
    )
    first_low = first_grad.astype(jnp.bfloat16)
    out_grad = jnp.einsum("td,te->de", context, first_low, preferred_element_type=jnp.float32)
    context_grad = (
        jnp.einsum("te,de->td", first_low, out_weight, preferred_element_type=jnp.float32)
        .astype(jnp.bfloat16)
        .reshape(head_shape)
    )
    row_delta = jnp.einsum("qhe,qhe->hq", context_grad.astype(jnp.float32), attended)
    query_grad, key_grad, value_grad = backward_cycle(
        query_heads,
        key_heads,
        value_heads,
        local_ids,
        every_id,
        context_grad,
        log_total,
        row_delta,
        cycle_place,
        cycle_size,
    )
    query_low = query_grad.astype(jnp.bfloat16).reshape(frame_count, model_width)
    key_low = key_grad.astype(jnp.bfloat16).reshape(frame_count, model_width)
    value_low = value_grad.astype(jnp.bfloat16).reshape(frame_count, model_width)
    proj_grad = jnp.concatenate([query_low, key_low, value_low], axis=1)
    qkv_grad = jnp.einsum("td,te->de", inputs, proj_grad, preferred_element_type=jnp.float32)
    input_grad = (
        jnp.einsum("te,de->td", proj_grad, qkv_weight, preferred_element_type=jnp.float32)
        + first_grad
    )
    summed = (
        lax.psum_scatter(qkv_grad, ("rows", "seq"), scatter_dimension=0, tiled=True),
        lax.psum_scatter(
            jnp.sum(query_low.astype(jnp.float32), axis=0),
            ("rows", "seq"),
            scatter_dimension=0,
            tiled=True,
        ),
        lax.psum_scatter(
            jnp.sum(value_low.astype(jnp.float32), axis=0),
            ("rows", "seq"),
            scatter_dimension=0,
            tiled=True,
        ),
        lax.psum_scatter(out_grad, ("rows", "seq"), scatter_dimension=0, tiled=True),
        lax.psum_scatter(
            jnp.sum(first_grad, axis=0), ("rows", "seq"), scatter_dimension=0, tiled=True
        ),
        lax.psum_scatter(gain_one_grad, ("rows", "seq"), scatter_dimension=0, tiled=True),
        lax.psum_scatter(shift_one_grad, ("rows", "seq"), scatter_dimension=0, tiled=True),
        lax.psum_scatter(up_grad, ("rows", "seq"), scatter_dimension=0, tiled=True),
        lax.psum_scatter(
            jnp.sum(pre_grad, axis=0), ("rows", "seq"), scatter_dimension=0, tiled=True
        ),
        lax.psum_scatter(down_grad, ("rows", "seq"), scatter_dimension=0, tiled=True),
        lax.psum_scatter(
            jnp.sum(second_grad, axis=0), ("rows", "seq"), scatter_dimension=0, tiled=True
        ),
        lax.psum_scatter(gain_two_grad, ("rows", "seq"), scatter_dimension=0, tiled=True),
        lax.psum_scatter(shift_two_grad, ("rows", "seq"), scatter_dimension=0, tiled=True),
    )
    return (
        output.astype(jnp.bfloat16)[None],
        input_grad[None],
        summed[0],
        summed[1],
        summed[2],
        summed[3],
        summed[4],
        summed[5],
        summed[6],
        summed[7],
        summed[8],
        summed[9],
        summed[10],
        summed[11],
        summed[12],
    )


HALF = HEAD_DIM
PAIRS = HEADS // 2
CONTRACT_LAST = (((1,), (1,)), ((), ()))
CONTRACT_INNER = (((1,), (0,)), ((), ()))
CONTRACT_FIRST = (((0,), (0,)), ((), ()))
IN_VMEM = pl.BlockSpec(memory_space=pltpu.VMEM)
IN_PLACE = pl.BlockSpec(memory_space=pl.ANY)
MESH_ID = pl.DeviceIdType.MESH
VMEM_BYTES = 60 << 20
BLOCKS = 16
PLANES = 4


def product(left, right, dims):
    return lax.dot_general(left, right, dims, preferred_element_type=jnp.float32)


def where_am_i():
    row = lax.axis_index("rows")
    place = lax.axis_index("seq")
    return row, place // 4, place // 2 % 2, place % 2


def meet(partners, count):
    barrier = pltpu.get_barrier_semaphore()
    for present, target in partners:

        def signal(target=target):
            pl.semaphore_signal(barrier, inc=1, device_id=target, device_id_type=MESH_ID)

        if present is None:
            signal()
        else:
            pl.when(present)(signal)
    pl.semaphore_wait(barrier, count)


class RowGather:
    UP, DOWN, ACROSS, BESIDE = range(4)

    def __init__(self, parts, line, crossing, sems):
        self.parts, self.line, self.crossing = parts, line, crossing
        self.recv_sem, self.beside_sem, self.line_sem, self.out_sem = sems
        self.row, self.z, self.x, self.c = where_am_i()
        self.has_up, self.has_down = self.z < PLANES - 1, self.z > 0
        self.far = (self.z + 2) % PLANES
        self.buffers = []
        for ref, _, _ in parts:
            if not any(ref is known for known in self.buffers):
                self.buffers.append(ref)

    def group(self, part):
        return [self.parts[part][0] is ref for ref in self.buffers].index(True)

    def device(self, z, x, c):
        return (self.row, z * 4 + x * 2 + c)

    def target(self, way):
        return (
            self.device(self.z + 1, self.x, self.c),
            self.device(self.z - 1, self.x, self.c),
            self.device(self.z, 1 - self.x, self.c),
            self.device(self.z, self.x, 1 - self.c),
        )[way]

    def copy(self, part, z, x, way):
        ref, first, rows = self.parts[part]
        piece = ref.at[z * 4 + x * 2 + self.c, pl.ds(first, rows)]
        beside = way == self.BESIDE
        return pltpu.make_async_remote_copy(
            src_ref=piece,
            dst_ref=piece,
            send_sem=self.out_sem.at[self.group(part)] if beside else self.line_sem.at[part, way],
            recv_sem=(
                self.beside_sem.at[self.group(part), z]
                if beside
                else self.recv_sem.at[part, z * 2 + x]
            ),
            device_id=self.target(way),
            device_id_type=MESH_ID,
        )

    def send(self, part, z, x, way):
        present = {self.UP: self.has_up, self.DOWN: self.has_down}.get(way)
        if present is None:
            self.copy(part, z, x, way).start()
        else:
            pl.when(present)(lambda: self.copy(part, z, x, way).start())

    def relay(self, part, z, x, ways, present=None):
        def both():
            self.copy(part, z, x, self.ACROSS).wait_recv()
            for way in ways:
                self.send(part, z, x, way)

        if present is None:
            both()
        else:
            pl.when(present)(both)

    def own(self):
        z, x = self.z, self.x
        for part in self.crossing:
            self.send(part, z, x, self.ACROSS)
        for part in self.line + self.crossing:
            self.send(part, z, x, self.UP)
            self.send(part, z, x, self.DOWN)
        for part in self.line:
            self.send(part, z, x, self.ACROSS)
        for part in self.crossing + self.line:
            self.send(part, z, x, self.BESIDE)

    def line_near(self):
        for part in self.line:
            self.relay(part, self.z - 1, self.x, (self.UP, self.ACROSS, self.BESIDE), self.has_down)
            self.relay(part, self.z + 1, self.x, (self.DOWN, self.ACROSS, self.BESIDE), self.has_up)

    def cross_over(self):
        for part in self.crossing:
            self.relay(part, self.z, 1 - self.x, (self.UP, self.DOWN, self.BESIDE))

    def cross_from(self, x):
        for part in self.crossing:
            self.relay(part, self.z - 1, x, (self.UP, self.BESIDE), self.has_down)
            self.relay(part, self.z + 1, x, (self.DOWN, self.BESIDE), self.has_up)

    def cross_near(self):
        self.cross_from(self.x)

    def cross_near_over(self):
        self.cross_from(1 - self.x)

    def line_over(self):
        for part in self.line:
            self.relay(part, self.z, 1 - self.x, (self.BESIDE,))

    def line_near_over(self):
        for part in self.line:
            self.relay(part, self.z - 1, 1 - self.x, (self.BESIDE,), self.has_down)
            self.relay(part, self.z + 1, 1 - self.x, (self.BESIDE,), self.has_up)

    def line_far(self):
        for part in self.line:
            self.relay(part, self.far, self.x, (self.ACROSS, self.BESIDE))

    def cross_far(self):
        for part in self.crossing:
            self.relay(part, self.far, self.x, (self.BESIDE,))

    def line_far_over(self):
        for part in self.line:
            self.relay(part, self.far, 1 - self.x, (self.BESIDE,))

    def cross_far_over(self):
        for part in self.crossing:
            self.relay(part, self.far, 1 - self.x, (self.BESIDE,))

    def plane_done(self, z, present=None):
        def wait():
            for i, ref in enumerate(self.buffers):
                both = ref.at[pl.ds(0, 2)]
                pltpu.make_async_remote_copy(
                    src_ref=both,
                    dst_ref=both,
                    send_sem=self.out_sem.at[i],
                    recv_sem=self.beside_sem.at[i, z],
                    device_id=self.target(self.BESIDE),
                    device_id_type=MESH_ID,
                ).wait_recv()

        if present is None:
            wait()
        else:
            pl.when(present)(wait)

    def left(self, sem, ref, count, first, rows):
        sent = ref.at[pl.ds(0, count), pl.ds(first, rows)]
        pltpu.make_async_remote_copy(
            src_ref=sent,
            dst_ref=sent,
            send_sem=sem,
            recv_sem=self.beside_sem.at[0, 0],
            device_id=self.target(self.BESIDE),
            device_id_type=MESH_ID,
        ).wait_send()

    def finish(self):
        def settle(ways, hops, planes):
            for part, (ref, first, rows) in enumerate(self.parts):
                wide = 1 if part in self.line else 2
                for way in ways:
                    self.left(self.line_sem.at[part, way], ref, wide * hops, first, rows)
                across = planes if part in self.line else 1
                self.left(self.line_sem.at[part, self.ACROSS], ref, across, first, rows)
            for i, ref in enumerate(self.buffers):
                self.left(self.out_sem.at[i], ref, 2 * planes, 0, ref.shape[1])

        pl.when(self.has_up & self.has_down)(lambda: settle((self.UP, self.DOWN), 2, 4))
        pl.when(jnp.logical_not(self.has_down))(lambda: settle((self.UP,), 1, 3))
        pl.when(jnp.logical_not(self.has_up))(lambda: settle((self.DOWN,), 1, 3))


def gather_sems(parts, groups):
    dma = pltpu.SemaphoreType.DMA
    return [dma((parts, 2 * PLANES)), dma((groups, PLANES)), dma((parts, 3)), dma((groups,))]


class VectorSum:
    STAGES = 5

    def __init__(self, ref, partial, arrived, send_sem, recv_sem):
        self.ref, self.partial, self.arrived = ref, partial, arrived
        self.send_sem, self.recv_sem = send_sem, recv_sem
        self.y, self.z, self.x, self.c = where_am_i()

    def copy(self, stage):
        y, z, x, c = self.y, self.z, self.x, self.c
        core, row, across, near, far = (
            (y, z, x, 1 - c),
            (1 - y, z, x, c),
            (y, z, 1 - x, c),
            (y, z + 1 - 2 * (z % 2), x, c),
            (y, (z + 2) % PLANES, x, c),
        )
        y, z, x, c = (core, row, across, near, far)[stage]
        return pltpu.make_async_remote_copy(
            src_ref=self.ref if stage == 0 else self.partial.at[stage - 1],
            dst_ref=self.arrived.at[stage],
            send_sem=self.send_sem.at[stage],
            recv_sem=self.recv_sem.at[stage],
            device_id=(y, z * 4 + x * 2 + c),
            device_id_type=MESH_ID,
        )

    def step(self, stage):
        if stage > 0:
            self.copy(stage - 1).wait_recv()
            before = self.ref[...] if stage == 1 else self.partial[stage - 2]
            self.partial[stage - 1] = before + self.arrived[stage - 1]
        if stage < self.STAGES:
            self.copy(stage).start()

    def finish(self):
        for stage in range(self.STAGES):
            self.copy(stage).wait_send()

    def own_share(self, rows, share):
        width = self.ref.shape[1]
        place = self.y * 16 + self.z * 4 + self.x * 2 + self.c
        per_row = width // share
        offset = place % per_row * share
        row_index = lax.broadcasted_iota(jnp.int32, (width, 128), 0)
        column_index = lax.broadcasted_iota(jnp.int32, (width, 128), 1)
        picked = jnp.where(
            (row_index == column_index + offset) & (column_index < share), 1.0, 0.0
        ).astype(jnp.bfloat16)
        rest = rows
        total = jnp.zeros((rows.shape[0], 128), jnp.float32)
        for _ in range(3):
            piece = rest.astype(jnp.bfloat16)
            total = total + product(piece, picked, CONTRACT_INNER)
            rest = rest - piece.astype(jnp.float32)
        return total, place // per_row


STEP = 384
KEY_STEPS = (384, 256, 128)
UNROLL = 6
CHUNK = 768


class CubeSum:
    STAGES = 3

    def __init__(self, partial, cube, line, send_sem, recv_sem):
        self.partial, self.cube, self.line = partial, cube, line
        self.send_sem, self.recv_sem = send_sem, recv_sem
        self.y, self.z, self.x, self.c = where_am_i()
        self.member = self.y * 4 + self.x * 2 + self.c

    def link(self, source, target, stage, device):
        return pltpu.make_async_remote_copy(
            src_ref=source,
            dst_ref=target,
            send_sem=self.send_sem.at[stage],
            recv_sem=self.recv_sem.at[stage],
            device_id=device,
            device_id_type=MESH_ID,
        )

    def others(self):
        for step in range(1, 8):
            other = (self.member + step) % 8
            yield (other // 4, self.z * 4 + other % 4)

    def copy(self, stage):
        beside = self.z + 1 - 2 * (self.z % 2) if stage == 1 else (self.z + 2) % PLANES
        return self.link(
            self.partial.at[stage - 1], self.line.at[stage - 1], stage,
            (self.y, beside * 4 + self.x * 2 + self.c),
        )

    def seven(self):
        seven = self.cube.at[pl.ds(0, 7)]
        return self.link(seven, seven, 0, (self.y, self.z * 4 + self.x * 2 + 1 - self.c))

    def step(self, stage):
        if stage == 0:
            own = self.cube.at[self.member]
            for device in self.others():
                self.link(own, own, 0, device).start()
            return
        if stage == 1:
            self.seven().wait_recv()
            self.partial[0] = jnp.sum(self.cube[...], axis=0)
        else:
            self.copy(stage - 1).wait_recv()
            self.partial[stage - 1] = self.partial[stage - 2] + self.line[stage - 2]
        if stage < self.STAGES:
            self.copy(stage).start()

    def finish(self):
        self.seven().wait_send()
        for stage in range(1, self.STAGES):
            self.copy(stage).wait_send()


class Quad:
    def __init__(self, by_x):
        self.by_x = by_x
        self.y, self.z, self.x, self.c = where_am_i()
        self.a, self.b = (self.x, self.y) if by_x else (self.y, self.x)
        self.mine = self.a * 2 + self.c
        self.peer = (1 - self.a) * 2 + self.c
        self.beside = self.a * 2 + 1 - self.c
        self.corner = (1 - self.a) * 2 + 1 - self.c

    def device(self, a, b, z, c):
        y, x = (b, a) if self.by_x else (a, b)
        return (y, z * 4 + x * 2 + c)

    def at_peer(self):
        return self.device(1 - self.a, self.b, self.z, self.c)

    def at_beside(self):
        return self.device(self.a, self.b, self.z, 1 - self.c)

    def at_corner(self):
        return self.device(1 - self.a, self.b, self.z, 1 - self.c)

    def link(self, source, target, send_sem, recv_sem, device):
        return pltpu.make_async_remote_copy(
            src_ref=source,
            dst_ref=target,
            send_sem=send_sem,
            recv_sem=recv_sem,
            device_id=device,
            device_id_type=MESH_ID,
        )

    def count(self, ref, send_sem, recv_sem):
        return self.link(ref, ref, send_sem, recv_sem, self.at_beside())


class Shared:
    def __init__(self, left, by_x, buffers):
        self.left = left
        self.held, self.send_sem, self.recv_sem = buffers
        self.quad = Quad(by_x)
        self.width = self.held.shape[2]

    def part(self, a):
        if self.quad.by_x:
            return self.left
        return self.left.at[:, pl.ds(pl.multiple_of(a * self.width, 128), self.width)]

    def share(self):
        q = self.quad
        slot = self.held.at[q.mine]
        send = self.send_sem.at[0]
        q.link(self.part(1 - q.a), slot, send, self.recv_sem.at[0], q.at_peer()).start()
        q.link(self.part(q.a), slot, send, self.recv_sem.at[1], q.at_beside()).start()
        self.held[q.mine] = self.part(q.a)[...]

    def relay(self):
        q = self.quad
        slot = self.held.at[q.peer]
        q.count(slot, self.send_sem.at[0], self.recv_sem.at[0]).wait_recv()
        q.link(slot, slot, self.send_sem.at[0], self.recv_sem.at[1], q.at_beside()).start()

    def complete(self):
        two = self.held.at[pl.ds(0, 2)]
        self.quad.count(two, self.send_sem.at[0], self.recv_sem.at[1]).wait_recv()

    def finish(self):
        three = self.held.at[pl.ds(0, 3)]
        self.quad.count(three, self.send_sem.at[0], self.recv_sem.at[1]).wait_send()


class Piece:
    def __init__(self, shared, right, base, stride, out, buffers):
        self.shared, self.right, self.base, self.stride, self.out = shared, right, base, stride, out
        self.rights, self.whole, self.b_in, self.z_in, self.last, self.send_sem, self.recv_sem = buffers
        self.wide = self.rights.shape[2]
        self.quad = shared.quad
        self.share_rows = out.shape[0]

    def columns(self, member):
        place = member if self.quad.by_x else member % 2
        return pl.ds(pl.multiple_of(self.base + place * self.stride, 128), self.wide)

    def give(self, member, device):
        self.quad.link(
            self.right.at[:, self.columns(member)], self.rights.at[self.quad.mine],
            self.send_sem.at[0], self.recv_sem.at[0], device,
        ).start()

    def share(self):
        q = self.quad
        self.give(q.peer, q.at_peer())
        self.give(q.corner, q.at_corner())
        self.give(q.beside, q.at_beside())
        self.rights[q.mine] = self.right[:, self.columns(q.mine)]

    def slab(self, b):
        return self.whole.at[b] if self.quad.by_x else self.whole.at[:, b]

    def cell(self, z):
        b = self.quad.b
        return self.whole.at[b, z] if self.quad.by_x else self.whole.at[z, b]

    def multiply(self):
        q = self.quad
        three = self.rights.at[pl.ds(0, 3)]
        q.count(three, self.send_sem.at[0], self.recv_sem.at[0]).wait_recv()
        held = self.shared.held
        tokens = held.shape[0] * held.shape[1]
        right = self.rights[...].reshape(tokens, self.wide)
        if self.shared.width > STEP:

            def one(i, carry):
                left = held[:, :, pl.ds(pl.multiple_of(i * STEP, 128), STEP)]
                part = product(left.reshape(tokens, STEP), right, CONTRACT_FIRST)
                self.whole[i] = part.astype(jnp.bfloat16).reshape(self.whole.shape[1:])
                return carry

            lax.fori_loop(0, self.shared.width // STEP, one, 0)
        else:
            part = product(held[...].reshape(tokens, STEP), right, CONTRACT_FIRST)
            self.whole[...] = part.astype(jnp.bfloat16).reshape(self.whole.shape)
        q.link(
            self.slab(1 - q.b), self.b_in, self.send_sem.at[1], self.recv_sem.at[1],
            q.device(q.a, 1 - q.b, q.z, q.c),
        ).start()

    def spread(self):
        q = self.quad
        q.count(self.b_in, self.send_sem.at[1], self.recv_sem.at[1]).wait_recv()
        slab = self.slab(q.b)
        slab[...] = (slab[...].astype(jnp.float32) + self.b_in[...].astype(jnp.float32)).astype(
            jnp.bfloat16
        )
        q.count(self.rights.at[pl.ds(0, 3)], self.send_sem.at[0], self.recv_sem.at[0]).wait_send()
        inner = self.inner()

        @pl.when(inner)
        def _():
            self.to_plane(self.cell(self.end()), 0, 1, self.end())

        @pl.when(jnp.logical_not(inner))
        def _():
            first = 1 - q.z // (PLANES - 1)
            three = pl.ds(first, 3)
            cells = self.whole.at[q.b, three] if q.by_x else self.whole.at[three, q.b]
            self.to_plane(cells, pl.ds(0, 3), 0, 1 + q.z // 2)

    def inner(self):
        return (self.quad.z > 0) & (self.quad.z < PLANES - 1)

    def end(self):
        return self.quad.z // 2 * (PLANES - 1)

    def to_plane(self, source, slot, which, z):
        q = self.quad
        q.link(
            source, self.z_in.at[slot], self.send_sem.at[0], self.recv_sem.at[2 + which],
            q.device(q.a, q.b, z, q.c),
        ).start()

    def fold(self):
        q = self.quad

        @pl.when(self.inner())
        def _():
            three = self.z_in.at[pl.ds(0, 3)]
            q.count(three, self.send_sem.at[0], self.recv_sem.at[2]).wait_recv()
            first = 2 - q.z
            for target in (PLANES - 1 - self.end(), PLANES - 1 - q.z):
                cell = self.cell(target)
                cell[...] = (
                    cell[...].astype(jnp.float32) + self.z_in[target - first].astype(jnp.float32)
                ).astype(jnp.bfloat16)
                self.to_plane(cell, 3, 1, target)

    def rows_of(self, member):
        place = member if self.quad.by_x else member % 2
        return self.last.at[pl.ds(pl.multiple_of(place * self.share_rows, 8), self.share_rows)]

    def collect(self):
        q = self.quad
        inner = self.inner()

        def arrived(count):
            some = self.z_in.at[pl.ds(0, count)]
            q.count(some, self.send_sem.at[0], self.recv_sem.at[3]).wait_recv()

        pl.when(inner)(lambda: arrived(1))
        pl.when(jnp.logical_not(inner))(lambda: arrived(2))
        beside = q.z // 2 * 2 * (1 - q.z // (PLANES - 1))
        self.last[...] = (
            self.cell(q.z)[...].astype(jnp.float32)
            + self.z_in[beside].astype(jnp.float32)
            + self.z_in[3].astype(jnp.float32)
        )
        q.count(self.b_in, self.send_sem.at[1], self.recv_sem.at[1]).wait_send()
        columns = self.out.at[:, self.columns(q.mine)]
        partners = [(q.beside, q.at_beside())]
        if q.by_x:
            partners = [(q.peer, q.at_peer()), (q.corner, q.at_corner())] + partners
        for member, device in partners:
            q.link(
                self.rows_of(member), columns, self.send_sem.at[1], self.recv_sem.at[4], device
            ).start()
        columns[...] = self.rows_of(q.mine)[...]

    def finish(self):
        q = self.quad
        others = self.last.at[pl.ds(0, (3 if q.by_x else 1) * self.share_rows)]
        q.count(others, self.send_sem.at[1], self.recv_sem.at[4]).wait()
        three = self.z_in.at[pl.ds(0, 3)]
        q.count(three, self.send_sem.at[0], self.recv_sem.at[2]).wait_send()


def shared_scratch(frame_count, left_width, by_x):
    return [
        pltpu.VMEM((4, frame_count, left_width if by_x else left_width // 2), jnp.bfloat16),
        pltpu.SemaphoreType.DMA((1,)),
        pltpu.SemaphoreType.DMA((2,)),
    ]


def piece_scratch(frame_count, left_width, by_x, wide=STEP):
    rows = left_width // (2 * PLANES) if by_x else left_width // (4 * PLANES)
    low = jnp.bfloat16
    return [
        pltpu.VMEM((4, frame_count, wide), low),
        pltpu.VMEM((2, PLANES, rows, wide) if by_x else (PLANES, 2, rows, wide), low),
        pltpu.VMEM((PLANES, rows, wide), low),
        pltpu.VMEM((PLANES, rows, wide), low),
        pltpu.VMEM((rows, wide), jnp.float32),
        pltpu.SemaphoreType.DMA((2,)),
        pltpu.SemaphoreType.DMA((5,)),
    ]


def cube_scratch(width):
    return [
        pltpu.VMEM((CubeSum.STAGES, 1, width), jnp.float32),
        pltpu.VMEM((8, 1, width), jnp.float32),
        pltpu.VMEM((CubeSum.STAGES - 1, 1, width), jnp.float32),
        pltpu.SemaphoreType.DMA((CubeSum.STAGES,)),
        pltpu.SemaphoreType.DMA((CubeSum.STAGES,)),
    ]


def vector_scratch(rows, width):
    wide = jnp.float32
    return [
        pltpu.VMEM((rows, width), wide),
        pltpu.VMEM((VectorSum.STAGES, rows, width), wide),
        pltpu.VMEM((VectorSum.STAGES, rows, width), wide),
        pltpu.SemaphoreType.DMA((VectorSum.STAGES,)),
        pltpu.SemaphoreType.DMA((VectorSum.STAGES,)),
    ]


def layer_scratch(frame_count, width, inner):
    low, wide = jnp.bfloat16, jnp.float32
    dma = pltpu.SemaphoreType.DMA
    return dict(
        qkv_held=pltpu.VMEM((width, 3 * width), low),
        out_held=pltpu.VMEM((width, width), low),
        up_held=pltpu.VMEM((width, inner), low),
        down_held=pltpu.VMEM((inner, width), low),
        weight_sem=dma((4,)),
        block=pltpu.VMEM((BLOCKS, frame_count + 16, width), low),
        block_sems=gather_sems(2, 1),
        grad_block=pltpu.VMEM((BLOCKS, frame_count, width), low),
        stats=pltpu.VMEM((BLOCKS, 32, frame_count), wide),
        grad_sems=gather_sems(3, 2),
        projected=pltpu.VMEM((BLOCKS, frame_count, 3 * width), low),
        mask=pltpu.VMEM((frame_count, BLOCKS * frame_count), wide),
        attended=pltpu.VMEM((frame_count, width), wide),
        slope=pltpu.VMEM((frame_count, inner), wide),
        logs=pltpu.VMEM((frame_count, 128), wide),
        delta=pltpu.VMEM((frame_count, 128), wide),
        inner_bias=pltpu.VMEM((1, inner), wide),
        proj_bias=pltpu.VMEM((1, 3 * width), wide),
        act=pltpu.VMEM((frame_count, inner), low),
        pre_low=pltpu.VMEM((frame_count, inner), low),
        context=pltpu.VMEM((frame_count, width), low),
        hidden_low=pltpu.VMEM((frame_count, width), low),
        second_low=pltpu.VMEM((frame_count, width), low),
        first_low=pltpu.VMEM((frame_count, width), low),
        normed=pltpu.VMEM((frame_count, width), wide),
        running=pltpu.VMEM((frame_count, width), wide),
        first_grad=pltpu.VMEM((frame_count, width), wide),
        proj_grad=pltpu.VMEM((frame_count, 3 * width), low),
        early=vector_scratch(16, width),
        late=cube_scratch(width),
        down_left=shared_scratch(frame_count, inner, False),
        up_left=shared_scratch(frame_count, width, True),
        out_left=shared_scratch(frame_count, width, False),
        qkv_left=shared_scratch(frame_count, width, False),
        down_piece=piece_scratch(frame_count, inner, False),
        up_pieces=[piece_scratch(frame_count, width, True) for _ in range(2)],
        out_piece=piece_scratch(frame_count, width, False),
        query_piece=piece_scratch(frame_count, width, False),
        key_pieces=[
            piece_scratch(frame_count, width, False, step) for step in KEY_STEPS
        ],
    )


class Inputs(typing.NamedTuple):
    frames: typing.Any
    segment_ids: typing.Any
    qkv_weight: typing.Any
    query_bias: typing.Any
    value_bias: typing.Any
    out_weight: typing.Any
    out_bias: typing.Any
    norm1_gain: typing.Any
    norm1_shift: typing.Any
    up_weight: typing.Any
    up_bias: typing.Any
    down_weight: typing.Any
    down_bias: typing.Any
    norm2_gain: typing.Any
    norm2_shift: typing.Any
    cotangent: typing.Any


class Outputs(typing.NamedTuple):
    layer_out: typing.Any
    input_grad: typing.Any
    qkv_g: typing.Any
    query_g: typing.Any
    value_g: typing.Any
    out_g: typing.Any
    outbias_g: typing.Any
    gain1_g: typing.Any
    shift1_g: typing.Any
    up_g: typing.Any
    upbias_g: typing.Any
    down_g: typing.Any
    downbias_g: typing.Any
    gain2_g: typing.Any
    shift2_g: typing.Any


class Refs:
    def __init__(self, *groups):
        for group in groups:
            for name, ref in group.items():
                setattr(self, name, ref)


def layer_kernel(held, *refs):
    inputs, outputs = len(Inputs._fields), len(Outputs._fields)
    scratch = jax.tree.unflatten(held, refs[inputs + outputs :])
    k = Refs(dict(zip(Inputs._fields + Outputs._fields, refs)), scratch)
    frame_count, width = k.frames.shape
    inner = k.inner_bias.shape[1]
    low, wide = jnp.bfloat16, jnp.float32
    total = BLOCKS * frame_count
    row, z, x, c = where_am_i()
    mine = z * 4 + x * 2 + c
    has_up, has_down = z < PLANES - 1, z > 0
    far = (z + 2) % PLANES
    lost = PLANES - 1 - z
    lane = lax.broadcasted_iota(jnp.int32, (frame_count, 128), 1)

    def fetch(i):
        source, target = (
            (k.qkv_weight, k.qkv_held),
            (k.out_weight, k.out_held),
            (k.up_weight, k.up_held),
            (k.down_weight, k.down_held),
        )[i]
        return pltpu.make_async_copy(source, target, k.weight_sem.at[i])

    for i in range(4):
        fetch(i).start()

    line_rows = frame_count * 80 // 128
    back_rows = frame_count * 64 // 128
    link = RowGather(
        [
            (k.block, 0, line_rows),
            (k.block, line_rows, k.block.shape[1] - line_rows),
        ],
        (0,),
        (1,),
        k.block_sems,
    )
    back = RowGather(
        [
            (k.grad_block, 0, back_rows),
            (k.grad_block, back_rows, frame_count - back_rows),
            (k.stats, 0, 32),
        ],
        (2, 0),
        (1,),
        k.grad_sems,
    )
    down_left = Shared(k.act, False, k.down_left)
    up_left = Shared(k.hidden_low, True, k.up_left)
    out_left = Shared(k.context, False, k.out_left)
    qkv_left = Shared(k.frames, False, k.qkv_left)
    half_width = width // 2
    down = Piece(down_left, k.second_low, 0, half_width, k.down_g, k.down_piece)
    ups = [
        Piece(up_left, k.pre_low, p * STEP, width, k.up_g, k.up_pieces[p]) for p in range(2)
    ]
    out = Piece(out_left, k.first_low, 0, half_width, k.out_g, k.out_piece)
    query = Piece(qkv_left, k.proj_grad, 0, half_width, k.qkv_g, k.query_piece)
    keys = [
        Piece(qkv_left, k.proj_grad, width + sum(KEY_STEPS[:i]), width, k.qkv_g, buffers)
        for i, buffers in enumerate(k.key_pieces)
    ]
    early, late = VectorSum(*k.early), CubeSum(*k.late)

    places = [(row, z, x, 1 - c), (1 - row, z, x, c), (1 - row, z, x, 1 - c)]
    places += [(row, z, 1 - x, c), (row, z, 1 - x, 1 - c)]
    places += [(1 - row, z, 1 - x, c), (1 - row, z, 1 - x, 1 - c)]
    places += [(row, (z + 2) % PLANES, x, c), (row, z + 1 - 2 * (z % 2), x, c)]
    partners = [(None, (y, at * 4 + across * 2 + core)) for y, at, across, core in places]
    middle = has_up & has_down
    partners.append((middle, (row, (PLANES - 1 - z) * 4 + x * 2 + c)))
    meet(partners, len(places) + middle.astype(jnp.int32))

    own_ids = jnp.broadcast_to(k.segment_ids[...], (frame_count, frame_count)).astype(wide)
    ids_column = own_ids.T
    k.block[mine, pl.ds(0, frame_count), :] = k.frames[...]
    k.block[mine, pl.ds(frame_count, 16), pl.ds(0, frame_count)] = own_ids[:16].astype(low)
    link.own()
    link.cross_over()
    link.line_near()
    k.inner_bias[...] = k.up_bias[...].reshape(1, inner)
    query_bias = k.query_bias[...].reshape(1, width)
    k.proj_bias[...] = jnp.concatenate(
        [query_bias, jnp.zeros((1, width), wide), k.value_bias[...].reshape(1, width)], axis=1
    )

    def plane_rows(plane):
        return jnp.concatenate(
            [k.block[plane * 4 + i, pl.ds(0, frame_count), :] for i in range(4)], axis=0
        )

    def project_columns(plane, first, count):
        def some(i, carry):
            columns = pl.ds(pl.multiple_of(first + i * CHUNK, 128), CHUNK)
            part = product(plane_rows(plane), k.qkv_held[:, columns], CONTRACT_INNER)
            part = (part + k.proj_bias[:, columns]).astype(low)
            if first == 0:
                part = part * HEAD_DIM**-0.5
            for b in range(4):
                k.projected[plane * 4 + b, :, columns] = part[
                    b * frame_count : (b + 1) * frame_count
                ]
            return carry

        lax.fori_loop(0, count // CHUNK, some, 0)

    def as_query(part):
        return (part + query_bias).astype(low) * HEAD_DIM**-0.5

    def project(plane):
        project_columns(plane, width, 2 * width)
        for i in range(4):
            ids = k.block[plane * 4 + i, pl.ds(frame_count, 8), pl.ds(0, frame_count)]
            same = jnp.broadcast_to(ids.astype(wide)[:1], own_ids.shape) == ids_column
            at = pl.multiple_of((plane * 4 + i) * frame_count, 128)
            k.mask[:, pl.ds(at, frame_count)] = jnp.where(same, 0.0, mask_fill)

    def project_queries(plane):
        project_columns(plane, 0, width)

    def queries_own_far():
        project_queries(z)
        project_queries(far)

    def queries_near():
        pl.when(has_down)(lambda: project_queries(z - 1))
        pl.when(has_up)(lambda: project_queries(z + 1))

    def planes_done():
        back.plane_done(z)
        back.plane_done(z - 1, has_down)
        back.plane_done(z + 1, has_up)
        back.plane_done(far)

    def input_gradient():
        k.input_grad[...] = k.first_grad[...] + product(
            k.proj_grad[...], k.qkv_held[...], CONTRACT_LAST
        )

    def query_note():
        note(early, 6, k.proj_grad[:, pl.ds(0, width)].astype(wide))

    def late_notes():
        values = k.proj_grad[:, pl.ds(2 * width, width)].astype(wide)
        late.cube[late.member] = jnp.sum(values, axis=0, keepdims=True)

    def small_shares():
        share = k.query_g.shape[0]
        first = early.partial[VectorSum.STAGES - 1]
        shares, _ = early.own_share(first[:8], share)
        k.query_g[...] = shares[6, :share]
        last = jnp.broadcast_to(late.partial[CubeSum.STAGES - 1], (8, width))
        k.value_g[...] = early.own_share(last, share)[0][0, :share]
        for i, ref in enumerate(
            (k.outbias_g, k.gain1_g, k.shift1_g, k.downbias_g, k.gain2_g, k.shift2_g)
        ):
            ref[...] = shares[i, :share]
        up_shares, at = early.own_share(first[8:], 4 * share)
        keep = lax.broadcasted_iota(jnp.int32, up_shares.shape, 0) == at
        picked = jnp.sum(jnp.where(keep, up_shares, 0.0), axis=0, keepdims=True)
        k.upbias_g[...] = picked[0, : 4 * share]

    def note(vector, index, values):
        vector.ref[pl.ds(index, 1), :] = jnp.sum(values, axis=0, keepdims=True)

    def flat(ref):
        return ref[...].reshape(1, width)

    def columns_of(third, j):
        return pl.ds(pl.multiple_of(third * width + j * 128, 128), 128)

    def head_state(h):
        return pl.ds(pl.multiple_of(h * 128, 128), 128)

    def both_heads(values):
        nothing = jnp.zeros_like(values)
        return jnp.concatenate(
            [jnp.where(lane < HALF, values, nothing), jnp.where(lane < HALF, nothing, values)],
            axis=0,
        )

    def own_halves(values):
        return jnp.where(lane < HALF, values[:frame_count], values[frame_count:])

    def attend(plane, first):
        at = pl.multiple_of(plane * 4 * frame_count, 128)

        def state(kind, j):
            return k.slope.at[:, pl.ds(pl.multiple_of((kind * HEADS + 2 * j) * 128, 128), 256)]

        def read(kind, j):
            pair_state = state(kind, j)[...]
            return jnp.concatenate([pair_state[:, :128], pair_state[:, 128:]], axis=0)

        def write(kind, j, values):
            state(kind, j)[...] = jnp.concatenate(
                [values[:frame_count], values[frame_count:]], axis=1
            )

        def pair(j, carry):
            query = both_heads(k.projected[mine, :, columns_of(0, j)])
            keys = k.projected[pl.ds(plane * 4, 4), :, columns_of(1, j)].reshape(-1, 128)
            values = k.projected[pl.ds(plane * 4, 4), :, columns_of(2, j)].reshape(-1, 128)
            mask = k.mask[:, pl.ds(at, 4 * frame_count)]
            scores = product(query, keys, CONTRACT_LAST) + jnp.concatenate([mask, mask], axis=0)
            tile = (2 * frame_count, 128)
            peak = jnp.broadcast_to(jnp.max(scores, axis=1, keepdims=True), tile)
            if not first:
                old = read(0, j)
                peak = jnp.maximum(peak, old)
                factor = jnp.exp(old - peak)
            weights = jnp.exp(scores - jnp.concatenate([peak] * 4, axis=1))
            whole = jnp.broadcast_to(jnp.sum(weights, axis=1, keepdims=True), tile)
            if not first:
                whole = whole + read(1, j) * factor
            write(0, j, peak)
            write(1, j, whole)
            both = own_halves(product(weights.astype(low), values, CONTRACT_INNER))
            if not first:
                both = both + k.attended[:, columns_of(0, j)] * own_halves(factor)
            k.attended[:, columns_of(0, j)] = both
            return carry

        lax.fori_loop(0, PAIRS, pair, 0, unroll=2 if first else UNROLL)

    def own_queries():
        fetch(0).wait()
        own = product(k.frames[...], k.qkv_held[:, pl.ds(0, width)], CONTRACT_INNER)
        k.projected[mine, :, pl.ds(0, width)] = as_query(own)

    def take_plane(plane, present=None):
        def take():
            link.plane_done(plane)
            project(plane)

        if present is None:
            take()
        else:
            pl.when(present)(take)

    def attend_near(plane, present):
        pl.when(present)(lambda: attend(plane, False))

    own_queries()
    link.line_over()
    take_plane(z)
    link.cross_near_over()
    link.cross_near()
    link.line_near_over()
    link.line_far()
    qkv_left.share()
    attend(z, True)
    take_plane(z - 1, has_down)
    take_plane(z + 1, has_up)
    link.line_far_over()
    link.cross_far()
    link.cross_far_over()
    attend_near(z + 1, has_up)
    attend_near(z - 1, has_down)
    take_plane(far)
    attend(far, False)
    logs = jnp.zeros(lane.shape, wide)
    for j in range(PAIRS):
        parts = []
        for h in range(2):
            whole = k.slope[:, head_state(HEADS + 2 * j + h)]
            logs = jnp.where(
                lane == 2 * j + h, k.slope[:, head_state(2 * j + h)] + jnp.log(whole), logs
            )
            parts.append(whole)
        done = k.attended[:, columns_of(0, j)] / jnp.where(lane < HALF, parts[0], parts[1])
        k.attended[:, columns_of(0, j)] = done
        k.context[:, columns_of(0, j)] = done.astype(low)
    k.logs[...] = logs

    def normalize(resid):
        centred = resid - jnp.mean(resid, axis=-1, keepdims=True)
        inverse = lax.rsqrt(jnp.mean(centred * centred, axis=-1, keepdims=True) + norm_eps)
        return centred * inverse, inverse

    def normalize_back(upstream, normed, inverse, gain):
        scaled = upstream * gain
        first_mean = jnp.mean(scaled, axis=-1, keepdims=True)
        second_mean = jnp.mean(scaled * normed, axis=-1, keepdims=True)
        return inverse * (scaled - first_mean - normed * second_mean)

    early.ref[...] = jnp.zeros((16, width), wide)
    fetch(1).wait()
    resid_one = (
        k.frames[...].astype(wide)
        + product(k.context[...], k.out_held[...], CONTRACT_INNER)
        + flat(k.out_bias)
    )
    normed_one, inverse_one = normalize(resid_one)
    k.normed[...] = normed_one
    hidden = normed_one * flat(k.norm1_gain) + flat(k.norm1_shift)
    k.hidden_low[...] = hidden.astype(low)
    up_left.share()
    k.running[...] = hidden + flat(k.down_bias)
    fetch(2).wait()
    fetch(3).wait()

    def forward(f, carry):
        columns = pl.ds(pl.multiple_of(f * width, 128), width)
        pre_act = (
            product(k.hidden_low[...], k.up_held[:, columns], CONTRACT_INNER)
            + k.inner_bias[:, columns]
        )
        normal_cdf = 0.5 * (1.0 + lax.erf(pre_act * 0.5**0.5))
        normal_pdf = jnp.exp(-0.5 * pre_act * pre_act) * (2.0 * math.pi) ** (-0.5)
        act = (pre_act * normal_cdf).astype(low)
        k.act[:, columns] = act
        k.slope[:, columns] = normal_cdf + pre_act * normal_pdf
        k.running[...] += product(
            act, k.down_held[pl.ds(pl.multiple_of(f * width, 128), width), :], CONTRACT_INNER
        )
        return carry

    lax.fori_loop(0, inner // width, forward, 0)
    down_left.share()
    out_left.share()
    normed_two, inverse_two = normalize(k.running[...])
    k.layer_out[...] = (normed_two * flat(k.norm2_gain) + flat(k.norm2_shift)).astype(low)
    upstream = k.cotangent[...].astype(wide)
    second_grad = normalize_back(upstream, normed_two, inverse_two, flat(k.norm2_gain))
    k.second_low[...] = second_grad.astype(low)
    note(early, 3, second_grad)
    note(early, 4, upstream * normed_two)
    note(early, 5, upstream)
    k.running[...] = second_grad

    def backward(p):
        for member in range(4):
            first = member * width + p * STEP
            columns = pl.ds(first, STEP)
            pre_grad = (
                product(k.second_low[...], k.down_held[columns, :], CONTRACT_LAST)
                * k.slope[:, columns]
            )
            early.ref[pl.ds(8 + member, 1), pl.ds(p * STEP, STEP)] = jnp.sum(
                pre_grad, axis=0, keepdims=True
            )
            k.pre_low[:, columns] = pre_grad.astype(low)
            k.running[...] += product(
                k.pre_low[:, columns], k.up_held[:, columns], CONTRACT_LAST
            )

    backward(0)
    ups[0].share()
    up_left.relay()
    backward(1)
    hidden_grad = k.running[...]
    normed_one = k.normed[...]
    first_grad = normalize_back(hidden_grad, normed_one, inverse_one, flat(k.norm1_gain))
    k.first_grad[...] = first_grad
    k.first_low[...] = first_grad.astype(low)
    note(early, 0, first_grad)
    note(early, 1, hidden_grad * normed_one)
    note(early, 2, hidden_grad)
    context_grad = product(k.first_low[...], k.out_held[...], CONTRACT_LAST).astype(low)
    k.grad_block[mine] = context_grad
    delta = jnp.zeros(lane.shape, wide)
    for j in range(PAIRS):
        columns = slice(j * 128, (j + 1) * 128)
        both = context_grad[:, columns].astype(wide) * k.attended[:, columns]
        for h in range(2):
            one = jnp.sum(
                jnp.where((lane < HALF) == (h == 0), both, 0.0), axis=1, keepdims=True
            )
            delta = jnp.where(lane == 2 * j + h, one, delta)
    k.delta[...] = delta
    k.stats[mine, pl.ds(0, 16), :] = k.logs[...].T[:16]
    k.stats[mine, pl.ds(16, 16), :] = delta.T[:16]
    down.share()
    back.own()

    @pl.when(jnp.logical_not(middle))
    def _():
        for i in range(4):
            k.projected[lost * 4 + i] = jnp.zeros((frame_count, 3 * width), low)
            k.grad_block[lost * 4 + i] = jnp.zeros((frame_count, width), low)
            k.stats[lost * 4 + i] = jnp.zeros((32, frame_count), wide)
            at = pl.multiple_of((lost * 4 + i) * frame_count, 128)
            k.mask[:, pl.ds(at, frame_count)] = jnp.full(lane.shape, mask_fill, wide)

    def query_pair(j):
        query = k.projected[mine, :, columns_of(0, j)]
        upstream = k.grad_block[mine, :, columns_of(0, j)]
        keys = k.projected[:, :, columns_of(1, j)].reshape(total, 128)
        values = k.projected[:, :, columns_of(2, j)].reshape(total, 128)
        outs = []
        for h in range(2):
            chosen = (lane < HALF) == (h == 0)
            nothing = jnp.zeros_like(query)
            logs = jnp.sum(
                jnp.where(lane == 2 * j + h, k.logs[...], 0.0), axis=1, keepdims=True
            )
            shift = jnp.sum(
                jnp.where(lane == 2 * j + h, k.delta[...], 0.0), axis=1, keepdims=True
            )
            scores = product(jnp.where(chosen, query, nothing), keys, CONTRACT_LAST)
            probs = jnp.exp(scores + k.mask[...] - logs)
            prob_grad = product(jnp.where(chosen, upstream, nothing), values, CONTRACT_LAST)
            score_grad = (probs * (prob_grad - shift)).astype(low)
            outs.append(product(score_grad, keys, CONTRACT_INNER))
        k.proj_grad[:, columns_of(0, j)] = (
            jnp.where(lane < HALF, outs[0], outs[1]) * HEAD_DIM**-0.5
        ).astype(low)

    def key_pair(j):
        key = k.projected[mine, :, columns_of(1, j)]
        value = k.projected[mine, :, columns_of(2, j)]
        queries = k.projected[:, :, columns_of(0, j)].reshape(total, 128)
        upstream = k.grad_block[:, :, columns_of(0, j)].reshape(total, 128)
        key_outs, value_outs = [], []
        for h in range(2):
            chosen = (lane < HALF) == (h == 0)
            nothing = jnp.zeros_like(key)
            logs = jnp.concatenate(
                [k.stats[b, pl.ds(2 * j + h, 1), :] for b in range(BLOCKS)], axis=1
            )
            shift = jnp.concatenate(
                [k.stats[b, pl.ds(16 + 2 * j + h, 1), :] for b in range(BLOCKS)], axis=1
            )
            scores = product(jnp.where(chosen, key, nothing), queries, CONTRACT_LAST)
            probs = jnp.exp(scores + k.mask[...] - logs)
            prob_grad = product(jnp.where(chosen, value, nothing), upstream, CONTRACT_LAST)
            score_grad = (probs * (prob_grad - shift)).astype(low)
            key_outs.append(product(score_grad, queries, CONTRACT_INNER))
            value_outs.append(product(probs.astype(low), upstream, CONTRACT_INNER))
        k.proj_grad[:, columns_of(1, j)] = jnp.where(
            lane < HALF, key_outs[0], key_outs[1]
        ).astype(low)
        k.proj_grad[:, columns_of(2, j)] = jnp.where(
            lane < HALF, value_outs[0], value_outs[1]
        ).astype(low)

    def pairs(one, first, last):
        def body(j, carry):
            one(j)
            return carry

        lax.fori_loop(first, last, body, 0)

    pairs(query_pair, 0, 3)
    back.cross_over()
    ups[1].share()
    pairs(query_pair, 3, 4)
    up_left.complete()
    back.line_near()
    down_left.relay()
    back.cross_near()
    pairs(query_pair, 4, 5)
    ups[0].multiply()
    back.line_far()
    down_left.complete()
    queries_own_far()
    back.cross_near_over()
    back.cross_far()
    back.line_near_over()
    ups[1].multiply()
    down.multiply()
    out_left.relay()
    queries_near()
    out.share()
    back.line_over()
    back.line_far_over()
    back.cross_far_over()
    ups[0].spread()
    pairs(query_pair, 5, 6)
    out_left.complete()
    planes_done()
    query_note()
    early.step(0)
    pairs(key_pair, 0, 1)
    qkv_left.relay()
    ups[1].spread()
    early.step(1)
    query.share()
    pairs(key_pair, 1, 2)
    qkv_left.complete()
    pairs(key_pair, 2, 3)
    ups[1].fold()
    ups[0].fold()
    pairs(key_pair, 3, 4)
    down.spread()
    out.multiply()
    early.step(2)
    pairs(key_pair, 4, 5)
    keys[0].share()
    pairs(key_pair, 5, 6)
    query.multiply()
    early.step(3)
    down.fold()
    keys[2].share()
    keys[1].share()
    out.spread()
    late_notes()
    late.step(0)
    input_gradient()
    keys[0].multiply()
    query.spread()
    out.fold()
    keys[2].multiply()
    early.step(4)
    keys[1].multiply()
    late.step(1)
    ups[0].collect()
    query.fold()
    down.collect()
    keys[0].spread()
    keys[0].fold()
    keys[2].spread()
    keys[1].spread()
    late.step(2)
    keys[2].fold()
    keys[1].fold()
    ups[1].collect()
    late.step(3)
    query.collect()
    keys[0].collect()
    early.step(5)
    out.collect()
    small_shares()
    keys[2].collect()
    keys[1].collect()
    for each in [down_left, up_left, out_left, qkv_left, down, out, query] + ups + keys:
        each.finish()
    for each in (back, link, early, late):
        each.finish()


def copy_kernel(*refs):
    count = len(refs) // 2
    for source, target in zip(refs[:count], refs[count:]):
        target[...] = source[...]


def hand_over(results):
    return pl.pallas_call(
        copy_kernel,
        out_shape=tuple(jax.ShapeDtypeStruct(each.shape, each.dtype) for each in results),
        in_specs=[IN_VMEM] * len(results),
        out_specs=(IN_VMEM,) * len(results),
    )(*results)


def layer_step(*args):
    frames = args[0]
    frame_count, width = frames.shape[1:]
    inner = args[9].shape[1]
    low, wide = jnp.bfloat16, jnp.float32
    scratch, held = jax.tree.flatten(layer_scratch(frame_count, width, inner))
    operands = [frames[0]] + list(args[1:-1]) + [args[-1][0]]
    share = width // 32
    shapes = [
        ((frame_count, width), low),
        ((frame_count, width), wide),
        ((share, 3 * width), wide),
        ((share,), wide),
        ((share,), wide),
        ((share, width), wide),
        ((share,), wide),
        ((share,), wide),
        ((share,), wide),
        ((share, inner), wide),
        ((4 * share,), wide),
        ((4 * share, width), wide),
        ((share,), wide),
        ((share,), wide),
        ((share,), wide),
    ]
    results = pl.pallas_call(
        functools.partial(layer_kernel, held),
        out_shape=tuple(jax.ShapeDtypeStruct(shape, kind) for shape, kind in shapes),
        in_specs=[IN_PLACE if each.ndim == 2 and each.shape[0] >= width else IN_VMEM for each in operands],
        out_specs=(IN_VMEM,) * len(shapes),
        scratch_shapes=scratch,
        compiler_params=pltpu.CompilerParams(
            collective_id=0, has_side_effects=True, vmem_limit_bytes=VMEM_BYTES
        ),
    )(*operands)
    results = hand_over(results)
    return (results[0][None], results[1][None]) + tuple(results[2:])


def solution(mesh):
    chosen = layer_step if dict(mesh.shape) == {"rows": 2, "seq": 16} else shards
    in_specs = (
        P("rows", "seq", None),
        P("rows", "seq"),
        P(),
        P(),
        P(),
        P(),
        P(),
        P(),
        P(),
        P(),
        P(),
        P(),
        P(),
        P(),
        P(),
        P("rows", "seq", None),
    )
    out_specs = (
        P("rows", "seq", None),
        P("rows", "seq", None),
        P(("rows", "seq"), None),
        P(("rows", "seq")),
        P(("rows", "seq")),
        P(("rows", "seq"), None),
        P(("rows", "seq")),
        P(("rows", "seq")),
        P(("rows", "seq")),
        P(("rows", "seq"), None),
        P(("rows", "seq")),
        P(("rows", "seq"), None),
        P(("rows", "seq")),
        P(("rows", "seq")),
        P(("rows", "seq")),
    )
    return jax.shard_map(chosen, mesh=mesh, in_specs=in_specs, out_specs=out_specs, check_vma=False)
```

profile of v0, /device:TPU:0, one launch (start us, length us, event | category | flops | bytes accessed | tf_op | source)
XLA Modules:
  0.0 101.1 jit_solution(7649024858390967402)
XLA Ops:
  0.7 97.7 %shard_map.271 = (bf16[128,768]{1,0:T(8,128)(2,1)}, f32[128,768]{1,0:T(8,128)}, f32[24,2304]{1,0:T(8,128)}, f32[24]{0:T(128)}, f32[24]{0:T(128)}, /*index=5*/f32...) custom-call(bf16[128,768]{1,0:T(8,128)(2,1)} %bitcast.4, ...), custom_call_target="tpu_custom_call" | custom-call | tf_op jit(solution)/shard_map/pallas_call | solution.py:1617
  98.4 2.5 %shard_map.272 = (bf16[128,768]{1,0:T(8,128)(2,1)}, f32[128,768]{1,0:T(8,128)}, f32[24,2304]{1,0:T(8,128)}, f32[24]{0:T(128)}, f32[24]{0:T(128)}, /*index=5*/f32...) custom-call(bf16[128,768]{1,0:T(8,128)(2,1)} %get-tuple-element.45.r, ...), custom_call_target="tpu_custom_call" | custom-call | tf_op jit(solution)/shard_map/pallas_call | solution.py:1584
where the time goes:
time: 101 us
  Pallas kernels  100 us (99%)
    pallas_call x1, Pallas kernels, layer_step(): pl.pallas_call(functools.partial(layer_kernel, held), out_shape=tuple((ja...  97.7 us
    pallas_call x1, Pallas kernels, hand_over(): pl.pallas_call(copy_kernel, out_shape=tuple((jax.ShapeDtypeStruct(each.sh...  2.55 us

commit v1 on v0

--- a/solution.py
+++ b/solution.py
@@ -958,6 +958,7 @@
         up_held=pltpu.VMEM((width, inner), low),
         down_held=pltpu.VMEM((inner, width), low),
         weight_sem=dma((4,)),
+        ready=pltpu.SemaphoreType.REGULAR,
         block=pltpu.VMEM((BLOCKS, frame_count + 16, width), low),
         block_sems=gather_sems(2, 1),
         grad_block=pltpu.VMEM((BLOCKS, frame_count, width), low),
@@ -1106,14 +1107,25 @@
     ]
     early, late = VectorSum(*k.early), CubeSum(*k.late)
 
+    middle = has_up & has_down
     places = [(row, z, x, 1 - c), (1 - row, z, x, c), (1 - row, z, x, 1 - c)]
     places += [(row, z, 1 - x, c), (row, z, 1 - x, 1 - c)]
-    places += [(1 - row, z, 1 - x, c), (1 - row, z, 1 - x, 1 - c)]
-    places += [(row, (z + 2) % PLANES, x, c), (row, z + 1 - 2 * (z % 2), x, c)]
     partners = [(None, (y, at * 4 + across * 2 + core)) for y, at, across, core in places]
-    middle = has_up & has_down
-    partners.append((middle, (row, (PLANES - 1 - z) * 4 + x * 2 + c)))
-    meet(partners, len(places) + middle.astype(jnp.int32))
+    partners += [
+        (has_up, (row, (z + 1) * 4 + x * 2 + c)),
+        (has_down, (row, (z - 1) * 4 + x * 2 + c)),
+    ]
+    meet(partners, len(places) + has_up.astype(jnp.int32) + has_down.astype(jnp.int32))
+
+    def tell(device):
+        pl.semaphore_signal(k.ready, inc=1, device_id=device, device_id_type=MESH_ID)
+
+    tell((row, z * 4 + (1 - x) * 2 + c))
+
+    @pl.when(middle)
+    def _():
+        tell((row, (z + 1) * 4 + x * 2 + c))
+        tell((row, (z - 1) * 4 + x * 2 + c))
 
     own_ids = jnp.broadcast_to(k.segment_ids[...], (frame_count, frame_count)).astype(wide)
     ids_column = own_ids.T
@@ -1417,6 +1429,7 @@
     k.stats[mine, pl.ds(16, 16), :] = delta.T[:16]
     down.share()
     back.own()
+    pl.semaphore_wait(k.ready, 2)
 
     @pl.when(jnp.logical_not(middle))
     def _():

time: 101 us -> 101 us (level)
  no operation moved by 1% of the time
where the time goes in v1:
time: 101 us
  Pallas kernels  99.8 us (99%)
    pallas_call x1, Pallas kernels, layer_step(): pl.pallas_call(functools.partial(layer_kernel, held), out_shape=tuple((ja...  97.3 us
    pallas_call x1, Pallas kernels, hand_over(): pl.pallas_call(copy_kernel, out_shape=tuple((jax.ShapeDtypeStruct(each.sh...  2.55 us

profile of v1, /device:TPU:0, one launch (start us, length us, event | category | flops | bytes accessed | tf_op | source)
XLA Modules:
  0.0 100.7 jit_solution(7137785836133365307)
XLA Ops:
  0.7 97.3 %shard_map.271 = (bf16[128,768]{1,0:T(8,128)(2,1)}, f32[128,768]{1,0:T(8,128)}, f32[24,2304]{1,0:T(8,128)}, f32[24]{0:T(128)}, f32[24]{0:T(128)}, /*index=5*/f32...) custom-call(bf16[128,768]{1,0:T(8,128)(2,1)} %bitcast.4, ...), custom_call_target="tpu_custom_call" | custom-call | tf_op jit(solution)/shard_map/pallas_call | solution.py:1630
  98.0 2.5 %shard_map.272 = (bf16[128,768]{1,0:T(8,128)(2,1)}, f32[128,768]{1,0:T(8,128)}, f32[24,2304]{1,0:T(8,128)}, f32[24]{0:T(128)}, f32[24]{0:T(128)}, /*index=5*/f32...) custom-call(bf16[128,768]{1,0:T(8,128)(2,1)} %get-tuple-element.45.r, ...), custom_call_target="tpu_custom_call" | custom-call | tf_op jit(solution)/shard_map/pallas_call | solution.py:1597
